TPU v7x, 32 devices: a whole 2x2x4 slice. The times are simulated.
32 devices in a mesh: row: 4 (over z), col: 8 (over y, x, core).
Axes of the slice: x: 2, y: 2, z: 4, core: 2. Of those that a mesh axis runs over, the one named last changes fastest.
Arguments:
- factor_panel: bfloat16 [2, 1536, 24576], P(None, 'row', 'col'), may hold values from -0.0390625 to 0.0390625
- solved_trail: bfloat16 [24576, 384], P('col'), may hold values from -6 to 6
- right_sides: bfloat16 [2, 1536, 384], P(None, 'row'), may hold values from -6 to 6
- diag_inverse: bfloat16 [2, 1536, 1536], P(None, 'row'), may hold values from -1 to 1.5, as said below
- coupling: bfloat16 [1536, 1536], P('row'), may hold values from -0.15625 to 0.15625
Outputs:
- solution: bfloat16 [2, 1536, 384], P(None, 'row')
Inputs may be any that keep to these rules, and one draw needn't show every extreme that they name: Each diag_inverse[b] is upper triangular with a diagonal between 0.6 and 1.4.
All inputs are finite; a program needn't handle non-finite values.
Results may differ from a plain program's by a relative error of at most 0.0057.
Values may be sent and summed in bfloat16 or wider, within the bound.
A program may use at most 64 MiB of HBM per device.

v0:
```python
import jax
import jax.numpy as jnp
from jax import lax
from jax.sharding import PartitionSpec as P


def substitute(totals, rights, diag_inverse, coupling):
    next_res = (rights[1].astype(jnp.float32) - totals[1]).astype(jnp.bfloat16)
    columns = diag_inverse[1]
    next_sol = jnp.dot(
        columns,
        lax.all_gather(next_res, "row", axis=0, tiled=True),
        preferred_element_type=jnp.float32,
    ).astype(jnp.bfloat16)
    columns = coupling
    carried = jnp.dot(
        columns,
        lax.all_gather(next_sol, "row", axis=0, tiled=True),
        preferred_element_type=jnp.float32,
    )
    first_res = (rights[0].astype(jnp.float32) - totals[0] - carried).astype(jnp.bfloat16)
    columns = diag_inverse[0]
    first_sol = jnp.dot(
        columns,
        lax.all_gather(first_res, "row", axis=0, tiled=True),
        preferred_element_type=jnp.float32,
    ).astype(jnp.bfloat16)
    return jnp.stack([first_sol, next_sol])


def reduce_updates(factor_panel, trail_part):
    partial_value = jnp.einsum(
        "bik,kf->bif", factor_panel, trail_part, preferred_element_type=jnp.float32
    )
    return lax.psum(partial_value, "col")


def shards(factor_panel, solved_trail, right_sides, diag_inverse, coupling):
    totals = reduce_updates(factor_panel, solved_trail)
    return substitute(totals, right_sides, diag_inverse, coupling)


def solution(mesh):
    in_specs = (
        P(None, "row", "col"),
        P("col", None),
        P(None, "row", None),
        P(None, "row", None),
        P("row", None),
    )
    out_specs = P(None, "row", None)
    return jax.shard_map(shards, mesh=mesh, in_specs=in_specs, out_specs=out_specs, check_vma=False)
```

profile of v0, /device:TPU:0, one launch (start us, length us, event | category | flops | bytes accessed | tf_op | source)
XLA Modules:
  0.0 181.6 jit_solution(15904181698284857279)
XLA Ops:
  6.5 0.0 copy-start
  6.5 0.0 all-reduce.2.cloned.1.call-start
  6.5 1.7 copy-done
  8.2 5.9 %fusion = f32[2,384,384]{2,1,0:T(8,128)} fusion(bf16[2,384,3072]{2,1,0:T(8,128)(2,1)} %param.5, bf16[3072,384]{1,0:T(8,128)(2,1)S(1)} %copy-done), kind=kOutput, calls=%fused_computation | convolution fusion | flops 1811939328 | bytes 8257536 | tf_op jit(solution)/shard_map/bik,kf->bif/dot_general | solution.py:32
  14.1 0.0 copy-start.3
  14.2 0.0 all-reduce.2.cloned.1.call-update
  14.2 0.0 all-gather.9.cloned.1.call-start
  14.2 60.0 %all-reduce.2.cloned.1.call-done = f32[2,384,384]{2,1,0:T(8,128)} async-done(((f32[2,384,384]{2,1,0:T(8,128)}), f32[2,384,384]{2,1,0:T(8,128)}) %all-reduce.2.cloned.1.call-update) | async-done | bytes 1179664 | tf_op jit(solution)/shard_map/psum | solution.py:35
  74.3 0.0 copy-done.3
  74.3 1.8 %fusion.12 = bf16[1,384,384]{2,1,0:T(8,128)(2,1)} fusion(f32[2,384,384]{2,1,0:T(8,128)} %all-reduce.2.cloned.1.call-done, bf16[2,384,384]{2,1,0:T(8,128)(2,1)S(1)} %copy-done.3), kind=kLoop, calls=%fused_computation.14 | loop fusion | flops 442368 | bytes 1179648 | tf_op jit(solution)/shard_map/convert_element_type | solution.py:8
  76.1 0.0 all-gather.9.cloned.1.call-update
  76.1 0.0 copy-start.2
  76.1 0.0 all-gather.5.cloned.1.call-start
  76.2 29.6 %all-gather.9.cloned.1.call-done = bf16[1,1536,384]{2,1,0:T(8,128)(2,1)} async-done(((bf16[1,384,384]{2,1,0:T(8,128)(2,1)}), bf16[1,1536,384]{2,1,0:T(8,128)(2,1)}) %all-gather.9.cloned.1.call-update) | async-done | bytes 1179664 | tf_op jit(solution)/shard_map/all_gather | solution.py:12
  105.8 3.2 %convolution_convert_fusion.1 = bf16[384,384]{1,0:T(8,128)(2,1)} fusion(bf16[1,1536,384]{2,1,0:T(8,128)(2,1)} %all-gather.9.cloned.1.call-done, bf16[2,384,1536]{2,1,0:T(8,128)(2,1)} %param.8), kind=kOutput, calls=%fused_computation.5 | convolution fusion | flops 453132288 | bytes 2654208 | tf_op jit(solution)/shard_map/dot_general | solution.py:10
  108.9 0.0 all-gather.5.cloned.1.call-update
  109.0 0.0 all-gather.7.cloned.1.call-start
  109.0 29.5 %all-gather.5.cloned.1.call-done = bf16[1536,384]{0,1:T(8,128)(2,1)} async-done(((bf16[384,384]{0,1:T(8,128)(2,1)}), bf16[1536,384]{0,1:T(8,128)(2,1)}) %all-gather.5.cloned.1.call-update) | async-done | bytes 1179664 | tf_op jit(solution)/shard_map/all_gather | solution.py:18
  138.5 0.0 copy-done.2
  138.5 3.2 %fusion.3 = bf16[384,384]{1,0:T(8,128)(2,1)} fusion(bf16[1536,384]{0,1:T(8,128)(2,1)} %all-gather.5.cloned.1.call-done, bf16[384,1536]{1,0:T(8,128)(2,1)} %param.9, f32[2,384,384]{2,1,0:T(8,128)S(1)} %copy-done.2, bf16[2,384,384]{2,1,0:T(8,128)(2,1)} %param.7), kind=kOutput, calls=%fused_computation.6 | convolution fusion | flops 453574656 | bytes 3538944 | tf_op jit(solution)/shard_map/dot_general | solution.py:16
  141.7 0.0 all-gather.7.cloned.1.call-update
  141.7 0.0 copy-start.1
  141.7 29.7 %all-gather.7.cloned.1.call-done = bf16[1536,384]{1,0:T(8,128)(2,1)} async-done(((bf16[384,384]{1,0:T(8,128)(2,1)}), bf16[1536,384]{1,0:T(8,128)(2,1)}) %all-gather.7.cloned.1.call-update) | async-done | bytes 1179664 | tf_op jit(solution)/shard_map/all_gather | solution.py:25
  171.5 2.4 %fusion.9 = bf16[1,384,384]{1,2,0:T(8,128)(2,1)S(1)} fusion(bf16[1536,384]{1,0:T(8,128)(2,1)} %all-gather.7.cloned.1.call-done, bf16[2,384,1536]{2,1,0:T(8,128)(2,1)} %param.8), kind=kOutput, calls=%fused_computation.12 | convolution fusion | flops 453132288 | bytes 2654208 | tf_op jit(solution)/shard_map/dot_general | solution.py:23
  173.9 0.0 copy-done.1
  173.9 0.1 pad_maximum_fusion
  174.0 1.1 copy.6
Async XLA Ops:
  6.5 1.7 copy-start
  6.5 67.7 %all-reduce.2.cloned.1.call-start = ((), (), s32[]{:S(2)}) async-start(), calls=%async_computation | async-start | bytes 2359296 | tf_op jit(solution)/shard_map/psum | solution.py:35
  14.1 60.1 %copy-start.3 = (bf16[2,384,384]{2,1,0:T(8,128)(2,1)S(1)}, bf16[2,384,384]{2,1,0:T(8,128)(2,1)}, u32[]{:S(2)}) copy-start(bf16[2,384,384]{2,1,0:T(8,128)(2,1)} %param.7) | copy-start | bytes 1769476
  14.2 91.6 %all-gather.9.cloned.1.call-start = ((), (), s32[]{:S(2)}) async-start(), calls=%async_computation.3 | async-start | bytes 1474560 | tf_op jit(solution)/shard_map/all_gather | solution.py:12
  76.1 62.4 %copy-start.2 = (f32[2,384,384]{2,1,0:T(8,128)S(1)}, f32[2,384,384]{2,1,0:T(8,128)}, u32[]{:S(2)}) copy-start(f32[2,384,384]{2,1,0:T(8,128)} %all-reduce.2.cloned.1.call-done) | copy-start | bytes 3538948
  76.1 62.4 %all-gather.5.cloned.1.call-start = ((), (), s32[]{:S(2)}) async-start(), calls=%async_computation.1 | async-start | bytes 1474560 | tf_op jit(solution)/shard_map/all_gather | solution.py:18
  109.0 62.5 %all-gather.7.cloned.1.call-start = ((), (), s32[]{:S(2)}) async-start(), calls=%async_computation.2 | async-start | bytes 1474560 | tf_op jit(solution)/shard_map/all_gather | solution.py:25
  141.7 32.2 %copy-start.1 = (bf16[384,384]{1,0:T(8,128)(2,1)S(1)}, bf16[384,384]{1,0:T(8,128)(2,1)}, u32[]{:S(2)}) copy-start(bf16[384,384]{1,0:T(8,128)(2,1)} %convolution_convert_fusion.1) | copy-start | bytes 884740
Sparse Core Ops, SparseCore 0:
  14.3 59.9 all-reduce.1
  76.3 29.4 all-gather.8
  109.1 29.3 all-gather.4
  141.8 29.5 all-gather.6
where the time goes:
time: 182 us
  waiting for transfers between devices  149 us (82%)
  matrix products  14.7 us (8%)
  between operations  13.2 us (7%)
  local copies, waits for them, and re-layouts  2.74 us (2%)
  other arithmetic  1.9 us (1%)
    psum x1, waiting for transfers between devices, reduce_updates(): return lax.psum(partial_value, 'col')  60 us
    all_gather x1, waiting for transfers between devices, substitute(): lax.all_gather(first_res, 'row', axis=0, tiled=True)  29.7 us
    all_gather x1, waiting for transfers between devices, substitute(): lax.all_gather(next_res, 'row', axis=0, tiled=True)  29.6 us
    all_gather x1, waiting for transfers between devices, substitute(): lax.all_gather(next_sol, 'row', axis=0, tiled=True)  29.5 us
    dot_general x1, matrix products, reduce_updates(): jnp.einsum('bik,kf->bif', factor_panel, trail_part, preferred_element_typ...  5.95 us
  transfers between devices with their start and end apart: 4, of which 4 were waited for; matrix products, arithmetic and copies ran while one was open for 0% of the time, Pallas kernels for 0%

commit v1 on v0

--- a/solution.py
+++ b/solution.py
@@ -32,7 +32,7 @@
     partial_value = jnp.einsum(
         "bik,kf->bif", factor_panel, trail_part, preferred_element_type=jnp.float32
     )
-    return lax.psum(partial_value, "col")
+    return jnp.sum(lax.all_gather(partial_value, "col"), axis=0)
 
 
 def shards(factor_panel, solved_trail, right_sides, diag_inverse, coupling):

time: 182 us -> 188 us (1.033)
  other arithmetic: 1.9 us -> 6.07 us
  waiting for transfers between devices: 149 us -> 151 us
    all_gather x0 -> x1, waiting for transfers between devices: none -> 61.5 us  [reduce_updates(): return jnp.sum(lax.all_gather(partial_value, 'col'), axis=0)]
    psum x1 -> x0, waiting for transfers between devices: 60 us -> none  [reduce_updates(): return lax.psum(partial_value, 'col')]
    reduce_sum x0 -> x1, other arithmetic: none -> 4.26 us  [reduce_updates(): return jnp.sum(lax.all_gather(partial_value, 'col'), axis=0)]
where the time goes in v1:
time: 188 us
  waiting for transfers between devices  151 us (80%)
  matrix products  14.7 us (8%)
  between operations  13.2 us (7%)
  other arithmetic  6.07 us (3%)
  local copies, waits for them, and re-layouts  2.74 us (1%)
    all_gather x1, waiting for transfers between devices, reduce_updates(): return jnp.sum(lax.all_gather(partial_value, 'col'), axis=0)  61.5 us
    all_gather x1, waiting for transfers between devices, substitute(): lax.all_gather(next_res, 'row', axis=0, tiled=True)  30.4 us
    all_gather x1, waiting for transfers between devices, substitute(): lax.all_gather(first_res, 'row', axis=0, tiled=True)  29.8 us
    all_gather x1, waiting for transfers between devices, substitute(): lax.all_gather(next_sol, 'row', axis=0, tiled=True)  29.5 us
    dot_general x1, matrix products, reduce_updates(): jnp.einsum('bik,kf->bif', factor_panel, trail_part, preferred_element_typ...  5.95 us
    reduce_sum x1, other arithmetic, reduce_updates(): return jnp.sum(lax.all_gather(partial_value, 'col'), axis=0)  4.26 us
  transfers between devices with their start and end apart: 4, of which 4 were waited for; matrix products, arithmetic and copies ran while one was open for 0% of the time, Pallas kernels for 0%

profile of v1, /device:TPU:0, one launch (start us, length us, event | category | flops | bytes accessed | tf_op | source)
XLA Modules:
  0.0 188.0 jit_solution(11674395920280267553)
XLA Ops:
  6.5 0.0 copy-start
  6.5 0.0 all-gather.11.cloned.1.call-start
  6.5 1.7 copy-done
  8.2 6.0 %fusion = f32[2,384,384]{2,1,0:T(8,128)} fusion(bf16[2,384,3072]{2,1,0:T(8,128)(2,1)} %param.5, bf16[3072,384]{1,0:T(8,128)(2,1)S(1)} %copy-done), kind=kOutput, calls=%fused_computation | convolution fusion | flops 1811939328 | bytes 8257536 | tf_op jit(solution)/shard_map/bik,kf->bif/dot_general | solution.py:32
  14.2 0.0 all-gather.11.cloned.1.call-update
  14.2 0.0 all-gather.13.cloned.1.call-start
  14.2 61.5 %all-gather.11.cloned.1.call-done = f32[16,384,384]{2,1,0:T(8,128)} async-done(((f32[2,384,384]{2,1,0:T(8,128)}), f32[16,384,384]{2,1,0:T(8,128)}) %all-gather.11.cloned.1.call-update) | async-done | bytes 9437200 | tf_op jit(solution)/shard_map/all_gather | solution.py:35
  75.8 4.3 %reduce_sum.9 = f32[2,384,384]{2,1,0:T(8,128)S(1)} reduce(f32[8,2,384,384]{3,2,1,0:T(8,128)} %bitcast.36, f32[]{:T(128)} %constant.0.clone.1), dimensions={0}, to_apply=%region_0.0 | reduce | flops 2064384 | bytes 10616836 | tf_op jit(solution)/shard_map/reduce_sum | solution.py:35
  80.0 1.7 fusion.12
  81.8 0.0 all-gather.13.cloned.1.call-update
  81.8 0.0 all-gather.7.cloned.1.call-start
  81.8 30.4 %all-gather.13.cloned.1.call-done = bf16[1,1536,384]{2,1,0:T(8,128)(2,1)} async-done(((bf16[1,384,384]{2,1,0:T(8,128)(2,1)}), bf16[1,1536,384]{2,1,0:T(8,128)(2,1)}) %all-gather.13.cloned.1.call-update) | async-done | bytes 1179664 | tf_op jit(solution)/shard_map/all_gather | solution.py:12
  112.2 3.2 %convolution_convert_fusion.1 = bf16[384,384]{1,0:T(8,128)(2,1)} fusion(bf16[1,1536,384]{2,1,0:T(8,128)(2,1)} %all-gather.13.cloned.1.call-done, bf16[2,384,1536]{2,1,0:T(8,128)(2,1)} %param.8), kind=kOutput, calls=%fused_computation.5 | convolution fusion | flops 453132288 | bytes 2654208 | tf_op jit(solution)/shard_map/dot_general | solution.py:10
  115.4 0.0 all-gather.7.cloned.1.call-update
  115.4 0.0 all-gather.9.cloned.1.call-start
  115.4 29.5 %all-gather.7.cloned.1.call-done = bf16[1536,384]{0,1:T(8,128)(2,1)} async-done(((bf16[384,384]{0,1:T(8,128)(2,1)}), bf16[1536,384]{0,1:T(8,128)(2,1)}) %all-gather.7.cloned.1.call-update) | async-done | bytes 1179664 | tf_op jit(solution)/shard_map/all_gather | solution.py:18
  144.9 3.2 %fusion.3 = bf16[384,384]{1,0:T(8,128)(2,1)} fusion(bf16[1536,384]{0,1:T(8,128)(2,1)} %all-gather.7.cloned.1.call-done, bf16[384,1536]{1,0:T(8,128)(2,1)} %param.9, f32[2,384,384]{2,1,0:T(8,128)S(1)} %reduce_sum.9, bf16[2,384,384]{2,1,0:T(8,128)(2,1)} %param.7), kind=kOutput, calls=%fused_computation.6 | convolution fusion | flops 453574656 | bytes 3538944 | tf_op jit(solution)/shard_map/dot_general | solution.py:16
  148.1 0.0 all-gather.9.cloned.1.call-update
  148.1 0.0 copy-start.1
  148.1 29.8 %all-gather.9.cloned.1.call-done = bf16[1536,384]{1,0:T(8,128)(2,1)} async-done(((bf16[384,384]{1,0:T(8,128)(2,1)}), bf16[1536,384]{1,0:T(8,128)(2,1)}) %all-gather.9.cloned.1.call-update) | async-done | bytes 1179664 | tf_op jit(solution)/shard_map/all_gather | solution.py:25
  177.9 2.4 %fusion.9 = bf16[1,384,384]{1,2,0:T(8,128)(2,1)S(1)} fusion(bf16[1536,384]{1,0:T(8,128)(2,1)} %all-gather.9.cloned.1.call-done, bf16[2,384,1536]{2,1,0:T(8,128)(2,1)} %param.8), kind=kOutput, calls=%fused_computation.12 | convolution fusion | flops 453132288 | bytes 2654208 | tf_op jit(solution)/shard_map/dot_general | solution.py:23
  180.3 0.0 copy-done.1
  180.3 0.1 pad_maximum_fusion
  180.4 1.1 copy.7
Async XLA Ops:
  6.5 1.7 copy-start
  6.5 69.2 %all-gather.11.cloned.1.call-start = ((), (), s32[]{:S(2)}) async-start(), calls=%async_computation.2 | async-start | bytes 10616832 | tf_op jit(solution)/shard_map/all_gather | solution.py:35
  14.2 98.0 %all-gather.13.cloned.1.call-start = ((), (), s32[]{:S(2)}) async-start(), calls=%async_computation.3 | async-start | bytes 1474560 | tf_op jit(solution)/shard_map/all_gather | solution.py:12
  81.8 63.1 %all-gather.7.cloned.1.call-start = ((), (), s32[]{:S(2)}) async-start(), calls=%async_computation | async-start | bytes 1474560 | tf_op jit(solution)/shard_map/all_gather | solution.py:18
  115.4 62.5 %all-gather.9.cloned.1.call-start = ((), (), s32[]{:S(2)}) async-start(), calls=%async_computation.1 | async-start | bytes 1474560 | tf_op jit(solution)/shard_map/all_gather | solution.py:25
  148.1 32.2 %copy-start.1 = (bf16[384,384]{1,0:T(8,128)(2,1)S(1)}, bf16[384,384]{1,0:T(8,128)(2,1)}, u32[]{:S(2)}) copy-start(bf16[384,384]{1,0:T(8,128)(2,1)} %convolution_convert_fusion.1) | copy-start | bytes 884740
Sparse Core Ops, SparseCore 0:
  14.3 61.4 all-gather.10
  81.9 30.2 all-gather.12
  115.5 29.3 all-gather.6
  148.2 29.5 all-gather.8
